TPU v7x, 32 devices: a whole 2x2x4 slice. The times are simulated.
32 devices in a mesh: ab: 2 (over y), cd: 16 (over z, x, core).
Axes of the slice: x: 2, y: 2, z: 4, core: 2. Of those that a mesh axis runs over, the one named last changes fastest.
Arguments:
- amplitudes: float32 [768, 16384], P('cd', 'ab'), may hold values from -1.25 to 1.25
- driver: float32 [768, 16384], P('cd', 'ab'), may hold values from -6 to 6
- ladder: bfloat16 [16384, 16384], P('ab', 'cd'), may hold values from -0.125 to 0.125
- block_mask: int32 [128, 128], P('ab', 'cd'), may hold values 0 or 1
- pair_list: int32 [768], replicated, may hold values from 0 to 1023, as said below
- occ_energy: float32 [32], replicated, may hold values from -2 to -0.5
- virt_energy: float32 [128], replicated, may hold values from 0.5 to 3
Outputs:
- new_amplitudes: float32 [768, 16384], P('cd', 'ab')
Inputs may be any that keep to these rules, and one draw needn't show every extreme that they name: `pair_list`: the entries are distinct occupied pairs i * 32 + j. Rows come in aligned blocks of two: a pair with i != j shares its block with the pair (j, i); pairs with i == j stand two to a block. Pairs 0 and 1023 are always listed.
All inputs are finite; a program needn't handle non-finite values. No bound on the sum of `block_mask` on one device may be relied on, other than what follows from the above.
Results may differ from a plain program's by a relative error of at most 0.008.
Values may be sent and summed in bfloat16 or wider, within the bound.
A program may use at most 128 MiB of HBM per device.

v0:
```python
import jax
import jax.numpy as jnp
from jax import lax
from jax.sharding import PartitionSpec as P

NV = 128
NOCC = 32
BLK = 128
ITERS = 2


def swap_rows(values, diagonal_rows):
    row_count = values.shape[0]
    swapped = jnp.flip(values.reshape(row_count // 2, 2, -1), axis=1).reshape(row_count, -1)
    return jnp.where(diagonal_rows[:, None], values, swapped)


def flip_pairs(tiles, diagonal_rows, tile_width):
    row_count = tiles.shape[0]
    tile_count = tiles.shape[1]
    turned = jnp.swapaxes(tiles.reshape(row_count, tile_count, tile_width, tile_width), 2, 3)
    turned = turned.reshape(row_count, tile_count * tile_width * tile_width)
    return swap_rows(turned, diagonal_rows)


def body(amplitudes, driver, ladder, block_mask, pair_list, occ_energy, virt_energy):
    ab_count = lax.axis_size("ab")
    ab_index = lax.axis_index("ab")
    cd_index = lax.axis_index("cd")
    rows_dev, cols_dev = amplitudes.shape
    out_rows, in_cols = ladder.shape
    tile_width = NV // ab_count
    tile_area = tile_width * tile_width
    weights = ladder.reshape(out_rows // BLK, BLK, in_cols // BLK, BLK)
    weights = (weights * block_mask.astype(jnp.bfloat16)[:, None, :, None]).reshape(
        out_rows, in_cols
    )
    pairs_local = ab_index * cols_dev + jnp.arange(cols_dev, dtype=jnp.int32)
    big_a = pairs_local // (tile_width * NV)
    big_b = pairs_local // tile_area % ab_count
    first = big_a * tile_width + pairs_local // tile_width % tile_width
    second = big_b * tile_width + pairs_local % tile_width
    virt_index = jnp.arange(NV, dtype=jnp.int32)
    picks = (first[:, None] == virt_index).astype(jnp.float32) + (
        second[:, None] == virt_index
    ).astype(jnp.float32)
    col_energy = jnp.dot(picks, virt_energy, precision=lax.Precision.HIGHEST)
    row_pairs = lax.dynamic_slice_in_dim(pair_list, cd_index * rows_dev, rows_dev)
    occ_index = jnp.arange(NOCC, dtype=jnp.int32)
    occ_picks = (row_pairs[:, None] // NOCC == occ_index).astype(jnp.float32)
    occ_picks = occ_picks + (row_pairs[:, None] % NOCC == occ_index).astype(jnp.float32)
    row_energy = jnp.dot(occ_picks, occ_energy, precision=lax.Precision.HIGHEST)
    denominator = col_energy[None, :] - row_energy[:, None]
    local_diagonal = row_pairs // NOCC == row_pairs % NOCC
    turned_weights = jnp.swapaxes(
        weights.reshape(out_rows // tile_area, tile_width, tile_width, in_cols), 1, 2
    )
    turned_weights = turned_weights.reshape(out_rows, in_cols)
    state = amplitudes
    for step in range(ITERS):
        rounded = state.astype(jnp.bfloat16)
        regrouped = lax.all_to_all(rounded, "cd", split_axis=1, concat_axis=0, tiled=True)
        partial_value = lax.dot_general(
            lax.all_gather(regrouped, "ab", axis=1, tiled=True),
            weights,
            (((1,), (1,)), ((), ())),
            preferred_element_type=jnp.float32,
        )
        total = lax.psum_scatter(
            partial_value.astype(jnp.bfloat16), "cd", scatter_dimension=0, tiled=True
        ).astype(jnp.float32)
        tiles = lax.all_to_all(
            total.reshape(rows_dev, ab_count, tile_area).astype(jnp.bfloat16),
            "ab",
            split_axis=1,
            concat_axis=1,
            tiled=True,
        ).astype(jnp.float32)
        symmetric = total + flip_pairs(tiles, local_diagonal, tile_width)
        state = (driver + symmetric) / denominator
    return state


def solution(mesh):
    placed = (P("cd", "ab"), P("cd", "ab"), P("ab", "cd"), P("ab", "cd"), P(), P(), P())
    return jax.shard_map(body, mesh=mesh, in_specs=placed, out_specs=P("cd", "ab"), check_vma=False)
```

profile of v0, /device:TPU:0, one launch (start us, length us, event | category | flops | bytes accessed | tf_op | source)
XLA Modules:
  0.0 568.6 jit_solution(2987417950333544323)
XLA Ops:
  6.5 1.5 convert_element_type.47
  8.1 27.4 %all_to_all.48 = bf16[48,16,512]{2,0,1:T(8,128)(2,1)} all-to-all(bf16[48,16,512]{2,0,1:T(8,128)(2,1)S(1)} %bitcast.59), channel_id=1, replica_groups=mesh['ab'=2,'cd'=16] {'cd'}, dimensions={1} | all-to-all | bytes 1572864 | tf_op jit(solution)/shard_map/all_to_all | solution.py:62
  35.7 26.5 %all-gather.3.cloned.1.call-done = bf16[768,1024]{1,0:T(8,128)(2,1)} async-done(((bf16[768,512]{1,0:T(8,128)(2,1)}), bf16[768,1024]{1,0:T(8,128)(2,1)}) %all-gather.3.cloned.1.call-update) | async-done | bytes 1572880 | tf_op jit(solution)/shard_map/all_gather | solution.py:64
  62.2 6.1 %mul.31 = bf16[64,128,8,128]{3,2,1,0:T(8,128)(2,1)} broadcast(bf16[64,8]{1,0:T(8,128)(2,1)S(1)} %copy.52), dimensions={0,2} | broadcast | bytes 16778240 | tf_op jit(solution)/shard_map/mul | solution.py:35
  68.3 22.4 %fusion = bf16[768,8192]{0,1:T(8,128)(2,1)} fusion(bf16[768,1024]{1,0:T(8,128)(2,1)S(1)} %copy-done.3, bf16[8192,1024]{1,0:T(8,128)(2,1)} %param.9, bf16[1024,8,8,128]{3,2,1,0:T(8,128)(2,1)} %bitcast.51), kind=kOutput, calls=%fused_computation.3 | convolution fusion | flops 12899581952 | bytes 47710208 | tf_op jit(solution)/shard_map/dot_general | solution.py:63
  90.7 16.7 %copy.64 = bf16[768,8192]{1,0:T(8,128)(2,1)} copy(bf16[768,8192]{0,1:T(8,128)(2,1)} %fusion) | data formatting | bytes 25165824
  107.5 135.0 %reduce-scatter.7.cloned.1.call-done = bf16[48,8192]{1,0:T(8,128)(2,1)} async-done(((bf16[768,8192]{1,0:T(8,128)(2,1)}), bf16[48,8192]{1,0:T(8,128)(2,1)}) %reduce-scatter.7.cloned.1.call-update) | async-done | bytes 786448 | tf_op jit(solution)/shard_map/reduce_scatter | solution.py:69
  242.5 2.0 copy.65
  244.5 1.6 copy.55
  246.0 3.5 all-to-all-start.1
  250.6 6.4 %fusion.1 = f32[1,8192]{1,0:T(1,128)S(1)} fusion(s32[8192]{0:T(1024)S(1)} %get-tuple-element.9, s32[8192]{0:T(1024)S(1)} %get-tuple-element.8, f32[128]{0:T(128)S(1)} %copy-done), kind=kOutput, calls=%fused_computation.4 | convolution fusion | flops 17825792 | bytes 98816 | tf_op jit(solution)/shard_map/dot_general | solution.py:47
  257.0 2.8 all-to-all-done.1
  259.8 2.4 reshape.147
  262.2 2.4 copy.56
  264.6 1.9 reshape.142
  266.5 2.5 reshape_reshape.6
  269.0 26.0 %rev.7 = f32[24,2,8192]{2,1,0:T(2,128)S(1)} reverse(f32[24,2,8192]{2,1,0:T(2,128)} %reshape_reshape.6), dimensions={1} | reverse | bytes 3145728 | tf_op jit(solution)/shard_map/jit(_flip)/rev | solution.py:14
  295.0 1.1 reshape.143
  296.1 2.7 fusion.7
  298.9 25.1 %all_to_all.49 = bf16[48,16,512]{2,0,1:T(8,128)(2,1)} all-to-all(bf16[48,16,512]{2,0,1:T(8,128)(2,1)S(1)} %bitcast.60), channel_id=1, replica_groups=mesh['ab'=2,'cd'=16] {'cd'}, dimensions={1} | all-to-all | bytes 1572864 | tf_op jit(solution)/shard_map/all_to_all | solution.py:62
  324.1 25.6 %all-gather.5.cloned.1.call-done = bf16[768,1024]{1,0:T(8,128)(2,1)} async-done(((bf16[768,512]{1,0:T(8,128)(2,1)}), bf16[768,1024]{1,0:T(8,128)(2,1)}) %all-gather.5.cloned.1.call-update) | async-done | bytes 1572880 | tf_op jit(solution)/shard_map/all_gather | solution.py:64
  349.7 21.7 %convolution_convert_fusion = bf16[768,8192]{1,0:T(8,128)(2,1)} fusion(bf16[768,1024]{1,0:T(8,128)(2,1)} %all-gather.5.cloned.1.call-done, bf16[8192,1024]{1,0:T(8,128)(2,1)} %param.9, bf16[1024,8,8,128]{3,2,1,0:T(8,128)(2,1)} %bitcast.52), kind=kOutput, calls=%fused_computation.1 | convolution fusion | flops 12899581952 | bytes 47710208 | tf_op jit(solution)/shard_map/dot_general | solution.py:63
  371.5 135.0 %reduce-scatter.9.cloned.1.call-done = bf16[48,8192]{1,0:T(8,128)(2,1)} async-done(((bf16[768,8192]{1,0:T(8,128)(2,1)}), bf16[48,8192]{1,0:T(8,128)(2,1)}) %reduce-scatter.9.cloned.1.call-update) | async-done | bytes 786448 | tf_op jit(solution)/shard_map/reduce_scatter | solution.py:69
  506.5 2.0 copy.67
  509.3 12.7 %all_to_all.50 = bf16[48,2,4096]{2,0,1:T(8,128)(2,1)S(1)} all-to-all(bf16[48,2,4096]{2,0,1:T(8,128)(2,1)S(1)} %copy.61), channel_id=1, replica_groups=mesh['ab'=2,'cd'=16] {'ab'}, dimensions={1} | all-to-all | bytes 1572864 | tf_op jit(solution)/shard_map/all_to_all | solution.py:72
  522.0 2.4 reshape.148
  524.4 2.4 copy.62
  526.8 1.9 reshape.145
  528.7 2.5 reshape_reshape.7
  531.2 26.0 %rev.8 = f32[24,2,8192]{2,1,0:T(2,128)S(1)} reverse(f32[24,2,8192]{2,1,0:T(2,128)} %reshape_reshape.7), dimensions={1} | reverse | bytes 3145728 | tf_op jit(solution)/shard_map/jit(_flip)/rev | solution.py:14
  557.2 1.1 reshape.146
  558.3 3.8 subtract_divide_fusion
  (26 shorter events, 2.4 us)
Async XLA Ops:
  6.5 244.1 %copy-start = (f32[128]{0:T(128)S(1)}, f32[128]{0:T(128)}, u32[]{:S(2)}) copy-start(f32[128]{0:T(128)} %param.13) | copy-start | bytes 1540
  6.5 55.7 %all-gather.3.cloned.1.call-start = ((), (), s32[]{:S(2)}) async-start(), calls=%async_computation.6 | async-start | bytes 2359296 | tf_op jit(solution)/shard_map/all_gather | solution.py:64
  8.1 27.5 %copy-start.2 = (s32[64,8]{0,1:T(8,128)S(1)}, s32[64,8]{0,1:T(8,128)}, u32[]{:S(2)}) copy-start(s32[64,8]{0,1:T(8,128)} %param.10) | copy-start | bytes 6148
  35.6 206.9 %reduce-scatter.7.cloned.1.call-start = ((), (), s32[]{:S(2)}) async-start(), calls=%async_computation.8 | async-start | bytes 13369344 | tf_op jit(solution)/shard_map/reduce_scatter | solution.py:69
  62.2 6.1 %copy-start.3 = (bf16[768,1024]{1,0:T(8,128)(2,1)S(1)}, bf16[768,1024]{1,0:T(8,128)(2,1)}, u32[]{:S(2)}) copy-start(bf16[768,1024]{1,0:T(8,128)(2,1)} %all-gather.3.cloned.1.call-done) | copy-start | bytes 4718596
  244.4 5.9 %copy-start.4 = (f32[32]{0:T(128)S(1)}, f32[32]{0:T(128)}, u32[]{:S(2)}) copy-start(f32[32]{0:T(128)} %param.12) | copy-start | bytes 388
  246.0 13.8 %all-to-all-start.1 = ((bf16[48,2,4096]{2,0,1:T(8,128)(2,1)}), bf16[48,2,4096]{2,0,1:T(8,128)(2,1)S(1)}, u32[]{:S(2)}, u32[]{:S(2)}) async-start(bf16[48,2,4096]{2,0,1:T(8,128)(2,1)} %copy.55), calls=%async_computation.1 | async-start | bytes 1572864 | tf_op jit(solution)/shard_map/all_to_all | solution.py:72
  249.6 100.2 %all-gather.5.cloned.1.call-start = ((), (), s32[]{:S(2)}) async-start(), calls=%async_computation.7 | async-start | bytes 2359296 | tf_op jit(solution)/shard_map/all_gather | solution.py:64
  324.0 182.4 %reduce-scatter.9.cloned.1.call-start = ((), (), s32[]{:S(2)}) async-start(), calls=%async_computation.9 | async-start | bytes 13369344 | tf_op jit(solution)/shard_map/reduce_scatter | solution.py:69
  558.3 3.8 copy-start.1
Sparse Core Ops, SparseCore 0:
  35.7 26.4 all-gather.2
  107.5 134.9 reduce-scatter.6
  324.2 25.5 all-gather.4
  371.6 134.8 reduce-scatter.8
where the time goes:
time: 574 us; the launch traced here: 569 us
  waiting for transfers between devices  325 us (57%)
  local copies, waits for them, and re-layouts  102 us (18%)
  blocking collectives  65.3 us (11%)
  matrix products  50.7 us (9%)
  between operations  13.3 us (2%)
  other arithmetic  8.87 us (2%)
    reduce_scatter x2, waiting for transfers between devices, body(): lax.psum_scatter(partial_value.astype(jnp.bfloat16), 'cd', scatter_dimens...  270 us
    all_to_all x2, blocking collectives, body(): lax.all_to_all(rounded, 'cd', split_axis=1, concat_axis=0, tiled=True)  52.6 us
    all_gather x2, waiting for transfers between devices, body(): lax.all_gather(regrouped, 'ab', axis=1, tiled=True)  52.1 us
    rev x2, local copies, waits for them, and re-layouts, swap_rows(): jnp.flip(values.reshape(row_count // 2, 2, -1), axis=1)  51.9 us
    dot_general x2, matrix products, body(): lax.dot_general(lax.all_gather(regrouped, 'ab', axis=1, tiled=True), weig...  44.1 us
    unnamed x13, local copies, waits for them, and re-layouts  20.6 us
    all_to_all x1, blocking collectives, body(): lax.all_to_all(total.reshape(rows_dev, ab_count, tile_area).astype(jnp.bf...  12.7 us
  transfers between devices with their start and end apart: 5, of which 5 were waited for; matrix products, arithmetic and copies ran while one was open for 1% of the time, Pallas kernels for 0%

commit v1 on v0

--- a/solution.py
+++ b/solution.py
@@ -59,7 +59,10 @@
     state = amplitudes
     for step in range(ITERS):
         rounded = state.astype(jnp.bfloat16)
-        regrouped = lax.all_to_all(rounded, "cd", split_axis=1, concat_axis=0, tiled=True)
+        regrouped = jnp.concatenate(
+            lax.all_to_all(jnp.stack(jnp.split(rounded, lax.axis_size("cd"), axis=1)), "cd", 0, 0),
+            axis=0,
+        )
         partial_value = lax.dot_general(
             lax.all_gather(regrouped, "ab", axis=1, tiled=True),
             weights,

time: 574 us -> 553 us (0.963)
  local copies, waits for them, and re-layouts: 102 us -> 82.1 us
    unnamed x13 -> x40, local copies, waits for them, and re-layouts: 20.6 us -> 0.2 us
where the time goes in v1:
time: 553 us; the launch traced here: 548 us
  waiting for transfers between devices  325 us (59%)
  local copies, waits for them, and re-layouts  82.1 us (15%)
  blocking collectives  65.1 us (12%)
  matrix products  49.6 us (9%)
  between operations  13.5 us (2%)
  other arithmetic  8.87 us (2%)
    reduce_scatter x2, waiting for transfers between devices, body(): lax.psum_scatter(partial_value.astype(jnp.bfloat16), 'cd', scatter_dimens...  270 us
    all_to_all x2, blocking collectives, body(): lax.all_to_all(jnp.stack(jnp.split(rounded, lax.axis_size('cd'), axis=1))...  52.4 us
    all_gather x2, waiting for transfers between devices, body(): lax.all_gather(regrouped, 'ab', axis=1, tiled=True)  52 us
    rev x2, local copies, waits for them, and re-layouts, swap_rows(): jnp.flip(values.reshape(row_count // 2, 2, -1), axis=1)  51.9 us
    dot_general x2, matrix products, body(): lax.dot_general(lax.all_gather(regrouped, 'ab', axis=1, tiled=True), weig...  43 us
    all_to_all x1, blocking collectives, body(): lax.all_to_all(total.reshape(rows_dev, ab_count, tile_area).astype(jnp.bf...  12.7 us
  transfers between devices with their start and end apart: 5, of which 5 were waited for; matrix products, arithmetic and copies ran while one was open for 1% of the time, Pallas kernels for 0%

profile of v1, /device:TPU:0, one launch (start us, length us, event | category | flops | bytes accessed | tf_op | source)
XLA Modules:
  0.0 548.0 jit_solution(3819588129436561461)
XLA Ops:
  6.5 1.5 convert_element_type.43
  8.3 27.4 %all_to_all.20 = bf16[16,48,512]{2,1,0:T(8,128)(2,1)} all-to-all(bf16[16,48,512]{2,1,0:T(8,128)(2,1)S(1)} %constant_dynamic-update-slice_fusion), channel_id=1, replica_groups=mesh['ab'=2,'cd'=16] {'cd'}, dimensions={0} | all-to-all | bytes 1572864 | tf_op jit(solution)/shard_map/all_to_all | solution.py:63
  35.9 26.5 %all-gather.3.cloned.1.call-done = bf16[768,1024]{1,0:T(8,128)(2,1)} async-done(((bf16[768,512]{1,0:T(8,128)(2,1)}), bf16[768,1024]{1,0:T(8,128)(2,1)}) %all-gather.3.cloned.1.call-update) | async-done | bytes 1572880 | tf_op jit(solution)/shard_map/all_gather | solution.py:67
  62.4 6.1 %mul.31 = bf16[64,128,8,128]{3,2,1,0:T(8,128)(2,1)} broadcast(bf16[64,8]{1,0:T(8,128)(2,1)S(1)} %copy.19), dimensions={0,2} | broadcast | bytes 16778240 | tf_op jit(solution)/shard_map/mul | solution.py:35
  68.4 21.3 %convolution_convert_fusion.1 = bf16[768,8192]{1,0:T(8,128)(2,1)} fusion(bf16[768,1024]{1,0:T(8,128)(2,1)S(1)} %copy-done.3, bf16[8192,1024]{1,0:T(8,128)(2,1)} %param.9, bf16[1024,8,8,128]{3,2,1,0:T(8,128)(2,1)} %bitcast.171), kind=kOutput, calls=%fused_computation.2 | convolution fusion | flops 12899581952 | bytes 47710208 | tf_op jit(solution)/shard_map/dot_general | solution.py:66
  89.9 135.0 %reduce-scatter.3.cloned.1.call-done = bf16[48,8192]{1,0:T(8,128)(2,1)} async-done(((bf16[768,8192]{1,0:T(8,128)(2,1)}), bf16[48,8192]{1,0:T(8,128)(2,1)}) %reduce-scatter.3.cloned.1.call-update) | async-done | bytes 786448 | tf_op jit(solution)/shard_map/reduce_scatter | solution.py:72
  224.9 2.1 copy.34
  226.9 3.5 all-to-all-start.1
  230.5 0.8 fusion.28
  231.5 6.4 %fusion = f32[1,8192]{1,0:T(1,128)S(1)} fusion(s32[8192]{0:T(1024)S(1)} %get-tuple-element.9, s32[8192]{0:T(1024)S(1)} %get-tuple-element.8, f32[128]{0:T(128)S(1)} %copy-done), kind=kOutput, calls=%fused_computation.3 | convolution fusion | flops 17825792 | bytes 98816 | tf_op jit(solution)/shard_map/dot_general | solution.py:47
  237.9 2.8 all-to-all-done.1
  240.7 2.4 reshape.149
  243.1 2.4 copy.21
  245.5 2.6 reshape_reshape.6
  248.0 1.9 reshape.143
  249.9 26.0 %rev.7 = f32[24,2,8192]{2,1,0:T(2,128)S(1)} reverse(f32[24,2,8192]{2,1,0:T(2,128)} %reshape_reshape.6), dimensions={1} | reverse | bytes 3145728 | tf_op jit(solution)/shard_map/jit(_flip)/rev | solution.py:14
  275.9 1.1 reshape.144
  277.0 2.7 fusion.6
  279.9 25.0 %all_to_all.21 = bf16[16,48,512]{2,1,0:T(8,128)(2,1)} all-to-all(bf16[16,48,512]{2,1,0:T(8,128)(2,1)S(1)} %constant_dynamic-update-slice_fusion.16), channel_id=1, replica_groups=mesh['ab'=2,'cd'=16] {'cd'}, dimensions={0} | all-to-all | bytes 1572864 | tf_op jit(solution)/shard_map/all_to_all | solution.py:63
  304.9 0.2 reduce-scatter.5.cloned.1.call-start
  305.1 25.5 %all-gather.5.cloned.1.call-done = bf16[768,1024]{1,0:T(8,128)(2,1)} async-done(((bf16[768,512]{1,0:T(8,128)(2,1)}), bf16[768,1024]{1,0:T(8,128)(2,1)}) %all-gather.5.cloned.1.call-update) | async-done | bytes 1572880 | tf_op jit(solution)/shard_map/all_gather | solution.py:67
  330.6 21.7 %convolution_convert_fusion = bf16[768,8192]{1,0:T(8,128)(2,1)} fusion(bf16[768,1024]{1,0:T(8,128)(2,1)} %all-gather.5.cloned.1.call-done, bf16[8192,1024]{1,0:T(8,128)(2,1)} %param.9, bf16[1024,8,8,128]{3,2,1,0:T(8,128)(2,1)} %bitcast.172), kind=kOutput, calls=%fused_computation.1 | convolution fusion | flops 12899581952 | bytes 47710208 | tf_op jit(solution)/shard_map/dot_general | solution.py:66
  352.3 135.1 %reduce-scatter.5.cloned.1.call-done = bf16[48,8192]{1,0:T(8,128)(2,1)} async-done(((bf16[768,8192]{1,0:T(8,128)(2,1)}), bf16[48,8192]{1,0:T(8,128)(2,1)}) %reduce-scatter.5.cloned.1.call-update) | async-done | bytes 786448 | tf_op jit(solution)/shard_map/reduce_scatter | solution.py:72
  487.4 1.2 copy.33
  488.6 12.7 %all_to_all.22 = bf16[48,2,4096]{2,0,1:T(8,128)(2,1)S(1)} all-to-all(bf16[48,2,4096]{2,0,1:T(8,128)(2,1)S(1)} %bitcast.176), channel_id=1, replica_groups=mesh['ab'=2,'cd'=16] {'ab'}, dimensions={1} | all-to-all | bytes 1572864 | tf_op jit(solution)/shard_map/all_to_all | solution.py:75
  501.3 2.4 reshape.150
  503.7 2.4 copy.23
  506.1 2.6 reshape_reshape.7
  508.6 1.9 reshape.147
  510.5 26.0 %rev.8 = f32[24,2,8192]{2,1,0:T(2,128)S(1)} reverse(f32[24,2,8192]{2,1,0:T(2,128)} %reshape_reshape.7), dimensions={1} | reverse | bytes 3145728 | tf_op jit(solution)/shard_map/jit(_flip)/rev | solution.py:14
  536.5 1.1 reshape.148
  537.6 3.8 subtract_divide_fusion
  (53 shorter events, 0.8 us)
Async XLA Ops:
  6.5 225.0 %copy-start = (f32[128]{0:T(128)S(1)}, f32[128]{0:T(128)}, u32[]{:S(2)}) copy-start(f32[128]{0:T(128)} %param.13) | copy-start | bytes 1540
  6.5 55.8 %all-gather.3.cloned.1.call-start = ((), (), s32[]{:S(2)}) async-start(), calls=%async_computation.6 | async-start | bytes 2359296 | tf_op jit(solution)/shard_map/all_gather | solution.py:67
  8.1 27.6 %copy-start.2 = (s32[64,8]{0,1:T(8,128)S(1)}, s32[64,8]{0,1:T(8,128)}, u32[]{:S(2)}) copy-start(s32[64,8]{0,1:T(8,128)} %param.10) | copy-start | bytes 6148
  35.7 189.2 %reduce-scatter.3.cloned.1.call-start = ((), (), s32[]{:S(2)}) async-start(), calls=%async_computation.7 | async-start | bytes 13369344 | tf_op jit(solution)/shard_map/reduce_scatter | solution.py:72
  62.4 6.1 %copy-start.3 = (bf16[768,1024]{1,0:T(8,128)(2,1)S(1)}, bf16[768,1024]{1,0:T(8,128)(2,1)}, u32[]{:S(2)}) copy-start(bf16[768,1024]{1,0:T(8,128)(2,1)} %all-gather.3.cloned.1.call-done) | copy-start | bytes 4718596
  224.9 6.5 %copy-start.4 = (f32[32]{0:T(128)S(1)}, f32[32]{0:T(128)}, u32[]{:S(2)}) copy-start(f32[32]{0:T(128)} %param.12) | copy-start | bytes 388
  226.9 13.8 %all-to-all-start.1 = ((bf16[48,2,4096]{2,0,1:T(8,128)(2,1)}), bf16[48,2,4096]{2,0,1:T(8,128)(2,1)S(1)}, u32[]{:S(2)}, u32[]{:S(2)}) async-start(bf16[48,2,4096]{2,0,1:T(8,128)(2,1)} %bitcast.168), calls=%async_computation.2 | async-start | bytes 1572864 | tf_op jit(solution)/shard_map/all_to_all | solution.py:75
  230.5 100.1 %all-gather.5.cloned.1.call-start = ((), (), s32[]{:S(2)}) async-start(), calls=%async_computation.8 | async-start | bytes 2359296 | tf_op jit(solution)/shard_map/all_gather | solution.py:67
  304.9 182.5 %reduce-scatter.5.cloned.1.call-start = ((), (), s32[]{:S(2)}) async-start(), calls=%async_computation.9 | async-start | bytes 13369344 | tf_op jit(solution)/shard_map/reduce_scatter | solution.py:72
  537.6 3.8 copy-start.1
Sparse Core Ops, SparseCore 0:
  35.8 26.4 all-gather.2
  89.9 134.9 reduce-scatter.2
  305.0 25.5 all-gather.4
  352.5 134.9 reduce-scatter.4
